TPU v7x, 512 devices: a whole 4x8x8 slice. The times are simulated.
512 devices in a mesh: section: 8 (over z), tok: 64 (over y, x, core).
Axes of the slice: x: 4, y: 8, z: 8, core: 2. Of those that a mesh axis runs over, the one named last changes fastest.
Arguments:
- queries: bfloat16 [8, 16384, 4096], P('section', 'tok'), may hold values from -120 to 120
- suffix_kv: bfloat16 [8, 16384, 1024], P('section', 'tok'), may hold values from -4 to 4
- prefix_kv: bfloat16 [8, 64, 64, 1024], P('section', 'tok'), may hold values from -4 to 4
- served: int32 [8, 128, 8], P('section'), may hold values from -1 to 63, as said below
Outputs:
- passed: bfloat16 [8, 16384, 4096], P('section', 'tok')
Inputs may be any that keep to these rules, and one draw needn't show every extreme that they name: `served`: entry k of a row is -1 or a page in [k * 8, (k + 1) * 8); live entries come first, then -1; entry 0 is always live, and block 0 of every section has all 8 live.
All inputs are finite; a program needn't handle non-finite values.
Results may differ from a plain program's by a relative error of at most 0.0029.
Values may be sent and summed in bfloat16 or wider, within the bound.
No kernel may reach another device: no remote copies, remote signals or barrier semaphores. Data moves between devices by JAX's collectives and lax.ppermute only.
A program may use at most 64 MiB of HBM per device.

v0:
```python
import functools
import math

import jax
import jax.numpy as jnp
from jax import lax
from jax.experimental import pallas as pl
from jax.experimental.pallas import tpu as pltpu
from jax.sharding import PartitionSpec as P


Q_HEADS = 32
KV_HEADS = 4
GROUP = Q_HEADS // KV_HEADS
HEAD = 128
BLOCK = 128
PAGE = 64
DEPTH = 8
QB_DEV = 2
ROWS, CHIPS, CORES = 8, 4, 2
ROW_DEV = CHIPS * CORES
KEYS = DEPTH * PAGE + BLOCK

A_HEADS = (0, 1)
B_HEADS = (2, 3)


SMEM = functools.partial(pl.BlockSpec, memory_space=pltpu.SMEM)
VMEM = functools.partial(pl.BlockSpec, memory_space=pltpu.VMEM)


def next_section(x):
    n = lax.axis_size("section")
    return lax.ppermute(x, "section", [(i, (i + 1) % n) for i in range(n)])


def within_tok(x, chips=0, cores=0):
    pairs = []
    for row in range(ROWS):
        for chip in range(CHIPS):
            for core in range(CORES):
                there = (row * CHIPS + (chip + chips) % CHIPS) * CORES + (core + cores) % CORES
                pairs.append(((row * CHIPS + chip) * CORES + core, there))
    return lax.ppermute(x, "tok", pairs)


def across_rows(x):
    columns = [[row * ROW_DEV + at for row in range(ROWS)] for at in range(ROW_DEV)]
    return lax.all_to_all(x, "tok", 0, 0, axis_index_groups=columns, tiled=True)


def columns_of(heads):
    width = len(heads) * HEAD
    starts = (heads[0] * HEAD, (KV_HEADS + heads[0]) * HEAD)
    return [(i * width, (i + 1) * width, start, start + width) for i, start in enumerate(starts)]


def copies_kernel(columns, page, out):
    for to, to_end, start, end in columns:
        part = page[:, start:end]
        for i in range(out.shape[0]):
            out[i, :, to:to_end] = part


def stack_kernel(columns, *refs):
    out = refs[-1]
    for i, page in enumerate(refs[:-1]):
        for to, to_end, start, end in columns:
            out[i, :, to:to_end] = page[:, start:end]


def small_kernel(body, out_shape, *args):
    return pl.pallas_call(
        body,
        out_shape=out_shape,
        in_specs=[VMEM()] * len(args),
        out_specs=VMEM(),
        compiler_params=pltpu.CompilerParams(vmem_limit_bytes=4 << 20),
        cost_estimate=pl.CostEstimate(flops=0, transcendentals=0, bytes_accessed=1 << 20),
    )(*args)


def slot_of(served, block, level):
    pick = jnp.clip(served[block, level] - level * ROW_DEV, 0, ROW_DEV - 1)
    return pick >> 1, pick & (CORES - 1)


def place_of(tok):
    return tok >> 3, (tok >> 1) & (CHIPS - 1), tok & (CORES - 1)


def pick_for_rows_kernel(tok, served, mine, other, out):
    level, chip, core = place_of(tok[0])
    at = tok[0] & (ROW_DEV - 1)
    for row in range(ROWS):
        for b in range(QB_DEV):
            owner_chip, owner_core = slot_of(served, (row * ROW_DEV + at) * QB_DEV + b, level)
            back = (chip - owner_chip) & (CHIPS - 1)
            out[row, b] = lax.select_n(owner_core == core, other[back], mine[back])


def pick_for_rows(tok, served, mine, other):
    width = mine.shape[-1]
    return pl.pallas_call(
        pick_for_rows_kernel,
        out_shape=jax.ShapeDtypeStruct((ROWS, QB_DEV, PAGE, width), mine.dtype),
        in_specs=[SMEM(), SMEM(), VMEM(), VMEM()],
        out_specs=VMEM(),
        compiler_params=pltpu.CompilerParams(vmem_limit_bytes=16 << 20),
        cost_estimate=pl.CostEstimate(flops=0, transcendentals=0, bytes_accessed=4 << 20),
        name="pick_for_rows",
    )(tok, served, mine, other)


def pick_for_pair_kernel(tok, served, from0, from1, from2, from3, own, send):
    _, chip, _ = place_of(tok[0])
    for b in range(QB_DEV):
        for level in range(DEPTH):
            for whose, out in ((tok[0], own), (tok[0] ^ 1, send)):
                owner_chip, _ = slot_of(served, whose * QB_DEV + b, level)
                back = (chip - owner_chip) & (CHIPS - 1)
                even = lax.select_n(back == 2, from0[level], from2[level])
                odd = lax.select_n(back == 3, from1[level], from3[level])
                out[b, level] = lax.select_n((back & 1) == 1, even, odd)


def pick_for_pair(tok, served, sources):
    shape = jax.ShapeDtypeStruct((QB_DEV,) + sources[0].shape, sources[0].dtype)
    return pl.pallas_call(
        pick_for_pair_kernel,
        out_shape=(shape, shape),
        in_specs=[SMEM(), SMEM()] + [VMEM()] * CHIPS,
        out_specs=(VMEM(), VMEM()),
        compiler_params=pltpu.CompilerParams(vmem_limit_bytes=16 << 20),
        cost_estimate=pl.CostEstimate(flops=0, transcendentals=0, bytes_accessed=8 << 20),
        name="pick_for_pair",
    )(tok, served, *sources)


def attend(queries, own_keys, own_values, out, keys, values):
    keys[DEPTH * PAGE :, :] = own_keys[...]
    values[DEPTH * PAGE :, :HEAD] = own_values[...]
    values[DEPTH * PAGE :, HEAD:] = jnp.ones((BLOCK, HEAD), jnp.bfloat16)
    to_exp2 = math.log2(math.e) / math.sqrt(HEAD)
    row_index = lax.broadcasted_iota(jnp.int32, (BLOCK, BLOCK), 0)
    col_index = lax.broadcasted_iota(jnp.int32, (BLOCK, BLOCK), 1)
    causal = jnp.where(col_index <= row_index, 0.0, -jnp.inf)
    causal = jnp.concatenate([causal, causal], axis=0)

    def head(g):
        return slice(g * HEAD, (g + 1) * HEAD)

    def score(pair):
        rows = jnp.concatenate([queries[:, head(2 * pair)], queries[:, head(2 * pair + 1)]], axis=0)
        return lax.dot_general(
            rows, keys[...], (((1,), (1,)), ((), ())), preferred_element_type=jnp.float32
        )

    def weigh(scores):
        prefix = scores[:, : DEPTH * PAGE]
        own = scores[:, DEPTH * PAGE :] + causal
        top = jnp.maximum(
            jnp.max(prefix, axis=1, keepdims=True), jnp.max(own, axis=1, keepdims=True)
        )
        parts = [jnp.exp2((part - top) * to_exp2).astype(jnp.bfloat16) for part in (prefix, own)]
        return jnp.concatenate(parts, axis=1)

    def mix(pair, weights):
        mixed = jnp.dot(weights, values[...], preferred_element_type=jnp.float32)
        mixed = (mixed[:, :HEAD] / mixed[:, HEAD:]).astype(out.dtype)
        out[:, head(2 * pair)] = mixed[:BLOCK]
        out[:, head(2 * pair + 1)] = mixed[BLOCK:]

    pairs = GROUP // 2
    scores, weights = score(0), None
    for pair in range(pairs + 1):
        ahead = score(pair + 1) if pair + 1 < pairs else None
        now = weigh(scores) if pair < pairs else None
        if weights is not None:
            mix(pair - 1, weights)
        scores, weights = ahead, now


def attend_kernel(y_first, tok, served, *refs):
    if y_first:
        own_k, own_v, pair_k, pair_v, queries, own_keys, own_values = refs[:7]
    else:
        page_k, page_v, queries, own_keys, own_values = refs[:5]
    out, keys, values = refs[-3:]
    block = tok[0] * QB_DEV + pl.program_id(1)
    core = tok[0] & (CORES - 1)
    first = None
    for level in range(DEPTH):
        if y_first:
            here = slot_of(served, block, level)[1] == core
            key_rows = lax.select_n(here, pair_k[0, level], own_k[0, level])
            value_rows = lax.select_n(here, pair_v[0, level], own_v[0, level])
        else:
            key_rows, value_rows = page_k[level, 0], page_v[level, 0]
        live = served[block, level] >= 0
        first = key_rows if level == 0 else first
        rows = slice(level * PAGE, (level + 1) * PAGE)
        nothing = jnp.zeros((PAGE, HEAD), jnp.bfloat16)
        keys[rows, :] = lax.select_n(live, first, key_rows)
        values[rows, :HEAD] = lax.select_n(live, nothing, value_rows)
        values[rows, HEAD:] = lax.select_n(live, nothing, jnp.ones((PAGE, HEAD), jnp.bfloat16))
    attend(queries, own_keys, own_values, out, keys, values)


def attention(tok, served, pages, heads, queries, own_pairs, result):
    y_first = len(pages) == 2
    count, first = len(heads), heads[0]
    if y_first:
        page_block = (1, DEPTH, PAGE, HEAD)
        at = lambda part: pl.BlockSpec(page_block, lambda h, b: (b, 0, 0, part * count + h))
    else:
        page_block = (DEPTH, 1, PAGE, HEAD)
        at = lambda part: pl.BlockSpec(page_block, lambda h, b: (0, b, 0, part * count + h))
    wide = pl.BlockSpec((BLOCK, GROUP * HEAD), lambda h, b: (b, first + h))
    own = lambda part: pl.BlockSpec((BLOCK, HEAD), lambda h, b: (b, part * KV_HEADS + first + h))
    page_args, page_specs = [], []
    for page in pages:
        page_args += [page, page]
        page_specs += [at(0), at(1)]
    args = [tok, served] + page_args + [queries, own_pairs, own_pairs]
    specs = [SMEM(), SMEM()] + page_specs + [wide, own(0), own(1)]
    aliases = {}
    if result is not None:
        aliases = {len(args): 0}
        args.append(result)
        specs.append(pl.BlockSpec(memory_space=pl.ANY))
    items = count * QB_DEV * GROUP * BLOCK * KEYS
    return pl.pallas_call(
        functools.partial(attend_kernel, y_first),
        grid=(count, QB_DEV),
        out_shape=jax.ShapeDtypeStruct(queries.shape, queries.dtype),
        in_specs=specs,
        out_specs=wide,
        scratch_shapes=[pltpu.VMEM((KEYS, HEAD), jnp.bfloat16), pltpu.VMEM((KEYS, 2 * HEAD), jnp.bfloat16)],
        input_output_aliases=aliases,
        compiler_params=pltpu.CompilerParams(vmem_limit_bytes=24 << 20),
        cost_estimate=pl.CostEstimate(flops=items * 6 * HEAD, transcendentals=items, bytes_accessed=4 << 20),
        name="attend_b" if y_first else "attend_a",
    )(*args)


def on_device(queries, suffix_kv, prefix_kv, served):
    tok = lax.axis_index("tok").reshape(1)
    page = next_section(prefix_kv[0, 0])
    served = next_section(served[0])
    own_pairs = next_section(suffix_kv[0])
    queries = next_section(queries[0])

    def chip_copies(x):
        copies = [x]
        for d in range(1, CHIPS):
            copies.append(within_tok(x, chips=d))
        return copies

    width = 2 * len(B_HEADS) * HEAD
    level_b = small_kernel(
        functools.partial(copies_kernel, columns_of(B_HEADS)),
        jax.ShapeDtypeStruct((ROWS, PAGE, width), page.dtype),
        page,
    )
    level_b = across_rows(level_b)

    row_pages = chip_copies(page)
    width = 2 * len(A_HEADS) * HEAD
    mine = small_kernel(
        functools.partial(stack_kernel, columns_of(A_HEADS)),
        jax.ShapeDtypeStruct((CHIPS, PAGE, width), page.dtype),
        *row_pages,
    )
    other = within_tok(mine, cores=1)

    sent = pick_for_rows(tok, served, mine, other)
    pages = across_rows(sent.reshape(ROWS, QB_DEV * PAGE, width))
    pages = pages.reshape(DEPTH, QB_DEV, PAGE, width)

    sources = chip_copies(level_b)
    own, send = pick_for_pair(tok, served, sources)
    pair = within_tok(send, cores=1)
    result = attention(tok, served, (own, pair), B_HEADS, queries, own_pairs, None)
    result = attention(tok, served, (pages,), A_HEADS, queries, own_pairs, result)
    return result[None]


def solution(mesh):
    placed = (
        P("section", "tok", None),
        P("section", "tok", None),
        P("section", "tok", None, None),
        P("section", None, None),
    )
    return jax.shard_map(
        on_device, mesh=mesh, in_specs=placed, out_specs=P("section", "tok", None), check_vma=False
    )
```

profile of v0, /device:TPU:1, one launch (start us, length us, event | category | flops | bytes accessed | tf_op | source)
XLA Modules:
  0.0 155.2 jit_solution(486242379770208233)
XLA Ops:
  0.0 4.9 %collective-permute-start.1 = (bf16[64,1024]{1,0:T(8,128)(2,1)}, bf16[64,1024]{1,0:T(8,128)(2,1)S(1)}, u32[]{:S(2)}, u32[]{:S(2)}) collective-permute-start(bf16[64,1024]{1,0:T(8,128)(2,1)} %bitcast.14), channel_id=1, source_target_pairs={{0,64},{64,128},{128,192},{192,256},{256,320},{320,384},{384,448},... | collective-permute-start | bytes 393224 | tf_op jit(solution)/shard_map/ppermute | solution.py:34
  4.9 10.1 %collective-permute-done.1.refs_0_.page = bf16[64,1024]{1,0:T(8,128)(2,1)S(1)} collective-permute-done((bf16[64,1024]{1,0:T(8,128)(2,1)}, bf16[64,1024]{1,0:T(8,128)(2,1)S(1)}, u32[]{:S(2)}, u32[]{:S(2)}) %collective-permute-start.1) | collective-permute-done | bytes 131104 | tf_op jit(solution)/shard_map/ppermute | solution.py:34
  15.0 0.8 shard_map.47
  15.8 6.8 %all-to-all-start.1 = ((bf16[8,64,512]{2,1,0:T(8,128)(2,1)}), bf16[8,64,512]{2,1,0:T(8,128)(2,1)S(1)}, u32[]{:S(2)}, u32[]{:S(2)}) async-start(bf16[8,64,512]{2,1,0:T(8,128)(2,1)} %shard_map.47), calls=%async_computation.1 | async-start | bytes 1048576 | tf_op jit(solution)/shard_map/all_to_all | solution.py:49
  22.7 1.9 %collective-permute-start.6 = (bf16[256,4096]{1,0:T(8,128)(2,1)}, bf16[256,4096]{1,0:T(8,128)(2,1)S(1)}, u32[]{:S(2)}, u32[]{:S(2)}) collective-permute-start(bf16[256,4096]{1,0:T(8,128)(2,1)} %bitcast.12), channel_id=1, source_target_pairs={{0,64},{64,128},{128,192},{192,256},{256,320},{320,384},{384,448},... | collective-permute-start | bytes 6291464 | tf_op jit(solution)/shard_map/ppermute | solution.py:34
  24.6 4.4 %collective-permute-start.4 = (bf16[64,1024]{1,0:T(8,128)(2,1)S(1)}, bf16[64,1024]{1,0:T(8,128)(2,1)S(1)}, u32[]{:S(2)}, u32[]{:S(2)}) collective-permute-start(bf16[64,1024]{1,0:T(8,128)(2,1)S(1)} %collective-permute-done.1.refs_0_.page), channel_id=1, source_target_pairs={{0,6},{1,7},{2,0},{3,1},{4,2},{5,3},{6,4},{7,5},{8,14},{9,15},{10,... | collective-permute-start | bytes 393224 | tf_op jit(solution)/shard_map/ppermute | solution.py:44
  29.0 2.4 %collective-permute-start.3 = (bf16[64,1024]{1,0:T(8,128)(2,1)S(1)}, bf16[64,1024]{1,0:T(8,128)(2,1)S(1)}, u32[]{:S(2)}, u32[]{:S(2)}) collective-permute-start(bf16[64,1024]{1,0:T(8,128)(2,1)S(1)} %collective-permute-done.1.refs_0_.page), channel_id=1, source_target_pairs={{0,4},{1,5},{2,6},{3,7},{4,0},{5,1},{6,2},{7,3},{8,12},{9,13},{10,... | collective-permute-start | bytes 393224 | tf_op jit(solution)/shard_map/ppermute | solution.py:44
  31.4 2.5 %collective-permute-start.2 = (bf16[64,1024]{1,0:T(8,128)(2,1)S(1)}, bf16[64,1024]{1,0:T(8,128)(2,1)S(1)}, u32[]{:S(2)}, u32[]{:S(2)}) collective-permute-start(bf16[64,1024]{1,0:T(8,128)(2,1)S(1)} %collective-permute-done.1.refs_0_.page), channel_id=1, source_target_pairs={{0,2},{1,3},{2,4},{3,5},{4,6},{5,7},{6,0},{7,1},{8,10},{9,11},{10,... | collective-permute-start | bytes 393224 | tf_op jit(solution)/shard_map/ppermute | solution.py:44
  34.0 2.2 %collective-permute-done.3.refs_2_ = bf16[64,1024]{1,0:T(8,128)(2,1)S(1)} collective-permute-done((bf16[64,1024]{1,0:T(8,128)(2,1)S(1)}, bf16[64,1024]{1,0:T(8,128)(2,1)S(1)}, u32[]{:S(2)}, u32[]{:S(2)}) %collective-permute-start.3) | collective-permute-done | bytes 131104 | tf_op jit(solution)/shard_map/ppermute | solution.py:44
  36.2 4.0 %collective-permute-done.2.refs_1_ = bf16[64,1024]{1,0:T(8,128)(2,1)S(1)} collective-permute-done((bf16[64,1024]{1,0:T(8,128)(2,1)S(1)}, bf16[64,1024]{1,0:T(8,128)(2,1)S(1)}, u32[]{:S(2)}, u32[]{:S(2)}) %collective-permute-start.2) | collective-permute-done | bytes 131104 | tf_op jit(solution)/shard_map/ppermute | solution.py:44
  40.2 3.6 %collective-permute-start.5 = (bf16[4,64,512]{2,1,0:T(8,128)(2,1)S(1)}, bf16[4,64,512]{2,1,0:T(8,128)(2,1)S(1)}, u32[]{:S(2)}, u32[]{:S(2)}) collective-permute-start(bf16[4,64,512]{2,1,0:T(8,128)(2,1)S(1)} %shard_map.46.mine), channel_id=1, source_target_pairs={{0,1},{1,0},{2,3},{3,2},{4,5},{5,4},{6,7},{7,6},{8,9},{9,8},{10,11... | collective-permute-start | bytes 786440 | tf_op jit(solution)/shard_map/ppermute | solution.py:44
  43.9 1.9 %collective-permute-start = (s32[128,8]{1,0:T(8,128)S(1)}, s32[128,8]{1,0:T(8,128)S(1)}, u32[]{:S(2)}, u32[]{:S(2)}) collective-permute-start(s32[128,8]{1,0:T(8,128)S(1)} %bitcast.11), channel_id=1, source_target_pairs={{0,64},{64,128},{128,192},{192,256},{256,320},{320,384},{384,448},... | collective-permute-start | bytes 12296 | tf_op jit(solution)/shard_map/ppermute | solution.py:34
  45.8 27.2 %collective-permute-done.served = s32[128,8]{1,0:T(8,128)S(1)} collective-permute-done((s32[128,8]{1,0:T(8,128)S(1)}, s32[128,8]{1,0:T(8,128)S(1)}, u32[]{:S(2)}, u32[]{:S(2)}) %collective-permute-start) | collective-permute-done | bytes 4128 | tf_op jit(solution)/shard_map/ppermute | solution.py:34
  73.0 1.7 %pick_for_rows.1 = bf16[8,2,64,512]{3,2,1,0:T(8,128)(2,1)S(1)} custom-call(s32[1]{0:T(128)} %bitcast.tok, s32[128,8]{1,0:T(8,128)S(1)} %collective-permute-done.served, bf16[4,64,512]{2,1,0:T(8,128)(2,1)S(1)} %shard_map.46.mine, bf16[4,64,512]{2,1,0:T(8,128)(2,1)S(1)} %collective-permute-done.5.other), custom_call_target="tpu_custom_call" | custom-call | bytes 4194304 | tf_op jit(solution)/shard_map/pick_for_rows/pallas_call | solution.py:104
  74.8 1.0 copy-done.2
  75.8 0.8 copy-done.3
  76.6 6.4 %all-to-all-start = ((bf16[8,128,512]{2,1,0:T(8,128)(2,1)}), bf16[8,128,512]{2,1,0:T(8,128)(2,1)S(1)}, u32[]{:S(2)}, u32[]{:S(2)}) async-start(bf16[8,128,512]{2,1,0:T(8,128)(2,1)} %bitcast.10), calls=%async_computation | async-start | bytes 2097152 | tf_op jit(solution)/shard_map/all_to_all | solution.py:49
  82.9 4.4 %collective-permute-start.10 = (bf16[8,64,512]{2,1,0:T(8,128)(2,1)}, bf16[8,64,512]{2,1,0:T(8,128)(2,1)S(1)}, u32[]{:S(2)}, u32[]{:S(2)}) collective-permute-start(bf16[8,64,512]{2,1,0:T(8,128)(2,1)} %copy-done.3), channel_id=1, source_target_pairs={{0,6},{1,7},{2,0},{3,1},{4,2},{5,3},{6,4},{7,5},{8,14},{9,15},{10,... | collective-permute-start | bytes 1572872 | tf_op jit(solution)/shard_map/ppermute | solution.py:44
  87.3 2.4 %collective-permute-start.9 = (bf16[8,64,512]{2,1,0:T(8,128)(2,1)}, bf16[8,64,512]{2,1,0:T(8,128)(2,1)S(1)}, u32[]{:S(2)}, u32[]{:S(2)}) collective-permute-start(bf16[8,64,512]{2,1,0:T(8,128)(2,1)} %copy-done.3), channel_id=1, source_target_pairs={{0,4},{1,5},{2,6},{3,7},{4,0},{5,1},{6,2},{7,3},{8,12},{9,13},{10,... | collective-permute-start | bytes 1572872 | tf_op jit(solution)/shard_map/ppermute | solution.py:44
  89.8 2.5 %collective-permute-start.8 = (bf16[8,64,512]{2,1,0:T(8,128)(2,1)}, bf16[8,64,512]{2,1,0:T(8,128)(2,1)S(1)}, u32[]{:S(2)}, u32[]{:S(2)}) collective-permute-start(bf16[8,64,512]{2,1,0:T(8,128)(2,1)} %copy-done.3), channel_id=1, source_target_pairs={{0,2},{1,3},{2,4},{3,5},{4,6},{5,7},{6,0},{7,1},{8,10},{9,11},{10,... | collective-permute-start | bytes 1572872 | tf_op jit(solution)/shard_map/ppermute | solution.py:44
  92.3 4.5 %collective-permute-done.10.from3 = bf16[8,64,512]{2,1,0:T(8,128)(2,1)S(1)} collective-permute-done((bf16[8,64,512]{2,1,0:T(8,128)(2,1)}, bf16[8,64,512]{2,1,0:T(8,128)(2,1)S(1)}, u32[]{:S(2)}, u32[]{:S(2)}) %collective-permute-start.10) | collective-permute-done | bytes 524320 | tf_op jit(solution)/shard_map/ppermute | solution.py:44
  96.8 4.5 %collective-permute-done.9.from2 = bf16[8,64,512]{2,1,0:T(8,128)(2,1)S(1)} collective-permute-done((bf16[8,64,512]{2,1,0:T(8,128)(2,1)}, bf16[8,64,512]{2,1,0:T(8,128)(2,1)S(1)}, u32[]{:S(2)}, u32[]{:S(2)}) %collective-permute-start.9) | collective-permute-done | bytes 524320 | tf_op jit(solution)/shard_map/ppermute | solution.py:44
  101.2 14.8 %collective-permute-done.8.from1 = bf16[8,64,512]{2,1,0:T(8,128)(2,1)S(1)} collective-permute-done((bf16[8,64,512]{2,1,0:T(8,128)(2,1)}, bf16[8,64,512]{2,1,0:T(8,128)(2,1)S(1)}, u32[]{:S(2)}, u32[]{:S(2)}) %collective-permute-start.8) | collective-permute-done | bytes 524320 | tf_op jit(solution)/shard_map/ppermute | solution.py:44
  116.0 1.0 copy-done.4
  117.1 1.9 %pick_for_pair.1 = (bf16[2,8,64,512]{3,2,1,0:T(8,128)(2,1)S(1)}, bf16[2,8,64,512]{3,2,1,0:T(8,128)(2,1)S(1)}) custom-call(s32[1]{0:T(128)} %bitcast.tok, s32[128,8]{1,0:T(8,128)S(1)} %collective-permute-done.served, bf16[8,64,512]{2,1,0:T(8,128)(2,1)S(1)} %copy-done.4, bf16[8,64,512]{2,1,0:T(8,128)(2,1)S(1)} %collective-permute-done.8.from1, ...), custom_call_target="tpu_custom_call" | custom-call | bytes 8388608 | tf_op jit(solution)/shard_map/pick_for_pair/pallas_call | solution.py:129
  119.0 2.4 %collective-permute-start.11 = (bf16[2,8,64,512]{3,2,1,0:T(8,128)(2,1)S(1)}, bf16[2,8,64,512]{3,2,1,0:T(8,128)(2,1)S(1)}, u32[]{:S(2)}, u32[]{:S(2)}) collective-permute-start(bf16[2,8,64,512]{3,2,1,0:T(8,128)(2,1)S(1)} %get-tuple-element.8), channel_id=1, source_target_pairs={{0,1},{1,0},{2,3},{3,2},{4,5},{5,4},{6,7},{7,6},{8,9},{9,8},{10,11... | collective-permute-start | bytes 3145736 | tf_op jit(solution)/shard_map/ppermute | solution.py:44
  121.4 1.9 %collective-permute-start.7 = (bf16[256,1024]{1,0:T(8,128)(2,1)S(1)}, bf16[256,1024]{1,0:T(8,128)(2,1)S(1)}, u32[]{:S(2)}, u32[]{:S(2)}) collective-permute-start(bf16[256,1024]{1,0:T(8,128)(2,1)S(1)} %bitcast.13), channel_id=1, source_target_pairs={{0,64},{64,128},{128,192},{192,256},{256,320},{320,384},{384,448},... | collective-permute-start | bytes 1572872 | tf_op jit(solution)/shard_map/ppermute | solution.py:34
  123.3 14.6 %collective-permute-done.7.refs_5_.refs_6_.refs_3_.refs_4_ = bf16[256,1024]{1,0:T(8,128)(2,1)S(1)} collective-permute-done((bf16[256,1024]{1,0:T(8,128)(2,1)S(1)}, bf16[256,1024]{1,0:T(8,128)(2,1)S(1)}, u32[]{:S(2)}, u32[]{:S(2)}) %collective-permute-start.7) | collective-permute-done | bytes 524320 | tf_op jit(solution)/shard_map/ppermute | solution.py:34
  138.0 7.8 %attend_b.1.refs_5_ = bf16[256,4096]{1,0:T(8,128)(2,1)} custom-call(s32[1]{0:T(128)} %bitcast.tok, s32[128,8]{1,0:T(8,128)S(1)} %collective-permute-done.served, bf16[2,8,64,512]{3,2,1,0:T(8,128)(2,1)S(1)} %get-tuple-element.7.refs_0_.refs_1_, bf16[2,8,64,512]{3,2,1,0:T(8,128)(2,1)S(1)} %get-tuple-element.7.refs_0_.refs_1_, ...), custom_call_target="tpu_custom_call" | custom-call | flops 2013265920 | bytes 4194304 | tf_op jit(solution)/shard_map/attend_b/pallas_call | solution.py:233
  145.8 0.8 copy-done
  146.6 1.0 copy-done.1
  147.6 7.6 %attend_a.1 = bf16[256,4096]{1,0:T(8,128)(2,1)} custom-call(s32[1]{0:T(128)} %bitcast.tok, s32[128,8]{1,0:T(8,128)S(1)} %collective-permute-done.served, bf16[8,2,64,512]{3,2,1,0:T(8,128)(2,1)S(1)} %bitcast.8, bf16[8,2,64,512]{3,2,1,0:T(8,128)(2,1)S(1)} %bitcast.9, ...), custom_call_target="tpu_custom_call", output_to_operand_aliasing={{}: (7, {})} | custom-call | flops 2013265920 | bytes 4194304 | tf_op jit(solution)/shard_map/attend_a/pallas_call | solution.py:233
  (17 shorter events, 0.2 us)
Async XLA Ops:
  0.0 43.8 %copy-start.5 = (s32[1,128,8]{1,2,0:T(8,128)S(1)}, s32[1,128,8]{1,2,0:T(8,128)}, u32[]{:S(2)}) copy-start(s32[1,128,8]{1,2,0:T(8,128)} %param.7) | copy-start | bytes 12292
  0.0 15.0 %collective-permute-start.1 = (bf16[64,1024]{1,0:T(8,128)(2,1)}, bf16[64,1024]{1,0:T(8,128)(2,1)S(1)}, u32[]{:S(2)}, u32[]{:S(2)}) collective-permute-start(bf16[64,1024]{1,0:T(8,128)(2,1)} %bitcast.14), channel_id=1, source_target_pairs={{0,64},{64,128},{128,192},{192,256},{256,320},{320,384},{384,448},... | collective-permute-start | bytes 393224 | tf_op jit(solution)/shard_map/ppermute | solution.py:34
  15.8 59.9 %all-to-all-start.1 = ((bf16[8,64,512]{2,1,0:T(8,128)(2,1)}), bf16[8,64,512]{2,1,0:T(8,128)(2,1)S(1)}, u32[]{:S(2)}, u32[]{:S(2)}) async-start(bf16[8,64,512]{2,1,0:T(8,128)(2,1)} %shard_map.47), calls=%async_computation.1 | async-start | bytes 1048576 | tf_op jit(solution)/shard_map/all_to_all | solution.py:49
  22.7 115.3 %collective-permute-start.6 = (bf16[256,4096]{1,0:T(8,128)(2,1)}, bf16[256,4096]{1,0:T(8,128)(2,1)S(1)}, u32[]{:S(2)}, u32[]{:S(2)}) collective-permute-start(bf16[256,4096]{1,0:T(8,128)(2,1)} %bitcast.12), channel_id=1, source_target_pairs={{0,64},{64,128},{128,192},{192,256},{256,320},{320,384},{384,448},... | collective-permute-start | bytes 6291464 | tf_op jit(solution)/shard_map/ppermute | solution.py:34
  24.6 9.4 %collective-permute-start.4 = (bf16[64,1024]{1,0:T(8,128)(2,1)S(1)}, bf16[64,1024]{1,0:T(8,128)(2,1)S(1)}, u32[]{:S(2)}, u32[]{:S(2)}) collective-permute-start(bf16[64,1024]{1,0:T(8,128)(2,1)S(1)} %collective-permute-done.1.refs_0_.page), channel_id=1, source_target_pairs={{0,6},{1,7},{2,0},{3,1},{4,2},{5,3},{6,4},{7,5},{8,14},{9,15},{10,... | collective-permute-start | bytes 393224 | tf_op jit(solution)/shard_map/ppermute | solution.py:44
  29.0 7.2 %collective-permute-start.3 = (bf16[64,1024]{1,0:T(8,128)(2,1)S(1)}, bf16[64,1024]{1,0:T(8,128)(2,1)S(1)}, u32[]{:S(2)}, u32[]{:S(2)}) collective-permute-start(bf16[64,1024]{1,0:T(8,128)(2,1)S(1)} %collective-permute-done.1.refs_0_.page), channel_id=1, source_target_pairs={{0,4},{1,5},{2,6},{3,7},{4,0},{5,1},{6,2},{7,3},{8,12},{9,13},{10,... | collective-permute-start | bytes 393224 | tf_op jit(solution)/shard_map/ppermute | solution.py:44
  31.4 8.7 %collective-permute-start.2 = (bf16[64,1024]{1,0:T(8,128)(2,1)S(1)}, bf16[64,1024]{1,0:T(8,128)(2,1)S(1)}, u32[]{:S(2)}, u32[]{:S(2)}) collective-permute-start(bf16[64,1024]{1,0:T(8,128)(2,1)S(1)} %collective-permute-done.1.refs_0_.page), channel_id=1, source_target_pairs={{0,2},{1,3},{2,4},{3,5},{4,6},{5,7},{6,0},{7,1},{8,10},{9,11},{10,... | collective-permute-start | bytes 393224 | tf_op jit(solution)/shard_map/ppermute | solution.py:44
  40.2 32.9 %collective-permute-start.5 = (bf16[4,64,512]{2,1,0:T(8,128)(2,1)S(1)}, bf16[4,64,512]{2,1,0:T(8,128)(2,1)S(1)}, u32[]{:S(2)}, u32[]{:S(2)}) collective-permute-start(bf16[4,64,512]{2,1,0:T(8,128)(2,1)S(1)} %shard_map.46.mine), channel_id=1, source_target_pairs={{0,1},{1,0},{2,3},{3,2},{4,5},{5,4},{6,7},{7,6},{8,9},{9,8},{10,11... | collective-permute-start | bytes 786440 | tf_op jit(solution)/shard_map/ppermute | solution.py:44
  43.9 29.1 %collective-permute-start = (s32[128,8]{1,0:T(8,128)S(1)}, s32[128,8]{1,0:T(8,128)S(1)}, u32[]{:S(2)}, u32[]{:S(2)}) collective-permute-start(s32[128,8]{1,0:T(8,128)S(1)} %bitcast.11), channel_id=1, source_target_pairs={{0,64},{64,128},{128,192},{192,256},{256,320},{320,384},{384,448},... | collective-permute-start | bytes 12296 | tf_op jit(solution)/shard_map/ppermute | solution.py:34
  74.8 1.0 copy-start.2
  75.8 0.8 copy-start.3
  76.6 70.0 %all-to-all-start = ((bf16[8,128,512]{2,1,0:T(8,128)(2,1)}), bf16[8,128,512]{2,1,0:T(8,128)(2,1)S(1)}, u32[]{:S(2)}, u32[]{:S(2)}) async-start(bf16[8,128,512]{2,1,0:T(8,128)(2,1)} %bitcast.10), calls=%async_computation | async-start | bytes 2097152 | tf_op jit(solution)/shard_map/all_to_all | solution.py:49
  82.9 13.8 %collective-permute-start.10 = (bf16[8,64,512]{2,1,0:T(8,128)(2,1)}, bf16[8,64,512]{2,1,0:T(8,128)(2,1)S(1)}, u32[]{:S(2)}, u32[]{:S(2)}) collective-permute-start(bf16[8,64,512]{2,1,0:T(8,128)(2,1)} %copy-done.3), channel_id=1, source_target_pairs={{0,6},{1,7},{2,0},{3,1},{4,2},{5,3},{6,4},{7,5},{8,14},{9,15},{10,... | collective-permute-start | bytes 1572872 | tf_op jit(solution)/shard_map/ppermute | solution.py:44
  87.3 13.9 %collective-permute-start.9 = (bf16[8,64,512]{2,1,0:T(8,128)(2,1)}, bf16[8,64,512]{2,1,0:T(8,128)(2,1)S(1)}, u32[]{:S(2)}, u32[]{:S(2)}) collective-permute-start(bf16[8,64,512]{2,1,0:T(8,128)(2,1)} %copy-done.3), channel_id=1, source_target_pairs={{0,4},{1,5},{2,6},{3,7},{4,0},{5,1},{6,2},{7,3},{8,12},{9,13},{10,... | collective-permute-start | bytes 1572872 | tf_op jit(solution)/shard_map/ppermute | solution.py:44
  89.8 26.3 %collective-permute-start.8 = (bf16[8,64,512]{2,1,0:T(8,128)(2,1)}, bf16[8,64,512]{2,1,0:T(8,128)(2,1)S(1)}, u32[]{:S(2)}, u32[]{:S(2)}) collective-permute-start(bf16[8,64,512]{2,1,0:T(8,128)(2,1)} %copy-done.3), channel_id=1, source_target_pairs={{0,2},{1,3},{2,4},{3,5},{4,6},{5,7},{6,0},{7,1},{8,10},{9,11},{10,... | collective-permute-start | bytes 1572872 | tf_op jit(solution)/shard_map/ppermute | solution.py:44
  116.0 1.0 copy-start.4
  117.1 4.3 %copy-start.6 = (bf16[1,256,1024]{2,1,0:T(8,128)(2,1)S(1)}, bf16[1,256,1024]{2,1,0:T(8,128)(2,1)}, u32[]{:S(2)}) copy-start(bf16[1,256,1024]{2,1,0:T(8,128)(2,1)} %param.5) | copy-start | bytes 1572868
  119.0 19.0 %collective-permute-start.11 = (bf16[2,8,64,512]{3,2,1,0:T(8,128)(2,1)S(1)}, bf16[2,8,64,512]{3,2,1,0:T(8,128)(2,1)S(1)}, u32[]{:S(2)}, u32[]{:S(2)}) collective-permute-start(bf16[2,8,64,512]{3,2,1,0:T(8,128)(2,1)S(1)} %get-tuple-element.8), channel_id=1, source_target_pairs={{0,1},{1,0},{2,3},{3,2},{4,5},{5,4},{6,7},{7,6},{8,9},{9,8},{10,11... | collective-permute-start | bytes 3145736 | tf_op jit(solution)/shard_map/ppermute | solution.py:44
  121.4 16.6 %collective-permute-start.7 = (bf16[256,1024]{1,0:T(8,128)(2,1)S(1)}, bf16[256,1024]{1,0:T(8,128)(2,1)S(1)}, u32[]{:S(2)}, u32[]{:S(2)}) collective-permute-start(bf16[256,1024]{1,0:T(8,128)(2,1)S(1)} %bitcast.13), channel_id=1, source_target_pairs={{0,64},{64,128},{128,192},{192,256},{256,320},{320,384},{384,448},... | collective-permute-start | bytes 1572872 | tf_op jit(solution)/shard_map/ppermute | solution.py:34
  145.8 0.8 copy-start
  146.6 1.0 copy-start.1
where the time goes:
time: 156 us; the launch traced here: 155 us
  waiting for transfers between devices  81.9 us (53%)
  starting transfers between devices  48.5 us (31%)
  Pallas kernels  19.9 us (13%)
  local copies, waits for them, and re-layouts  4.77 us (3%)
    ppermute x4, waiting for transfers between devices, next_section(): return lax.ppermute(x, 'section', [(i, (i + 1) % n) for i in range(n)])  51.9 us
    ppermute x8, waiting for transfers between devices, within_tok(): return lax.ppermute(x, 'tok', pairs)  29.9 us
    ppermute x8, starting transfers between devices, within_tok(): return lax.ppermute(x, 'tok', pairs)  24.6 us
    pallas_call x2, Pallas kernels, attention(): pl.pallas_call(functools.partial(attend_kernel, y_first), grid=(count, QB...  15.4 us
    all_to_all x2, starting transfers between devices, across_rows(): return lax.all_to_all(x, 'tok', 0, 0, axis_index_groups=columns, tiled=True)  13.2 us
    ppermute x4, starting transfers between devices, next_section(): return lax.ppermute(x, 'section', [(i, (i + 1) % n) for i in range(n)])  10.7 us
    unnamed x15, local copies, waits for them, and re-layouts  4.77 us
  transfers between devices with their start and end apart: 14, of which 8 were waited for; matrix products, arithmetic and copies ran while one was open for 0% of the time, Pallas kernels for 7%

commit v1 on v0

--- a/solution.py
+++ b/solution.py
@@ -181,22 +181,27 @@
         scores, weights = ahead, now
 
 
-def attend_kernel(y_first, tok, served, *refs):
-    if y_first:
-        own_k, own_v, pair_k, pair_v, queries, own_keys, own_values = refs[:7]
-    else:
-        page_k, page_v, queries, own_keys, own_values = refs[:5]
+def attend_kernel(heads, y_first, tok, served, *refs):
+    pages, (queries, pairs) = refs[: 1 + y_first], refs[1 + y_first : 3 + y_first]
     out, keys, values = refs[-3:]
-    block = tok[0] * QB_DEV + pl.program_id(1)
+    count, first_head = len(heads), heads[0]
+    h, b = pl.program_id(0), pl.program_id(1)
+    block = tok[0] * QB_DEV + b
     core = tok[0] & (CORES - 1)
+
+    def columns(start, width=HEAD):
+        return pl.ds(pl.multiple_of(start * width, width), width)
+
+    def page_rows(level, part):
+        at = columns(part * count + h)
+        if not y_first:
+            return pages[0][level, b, :, at]
+        here = slot_of(served, block, level)[1] == core
+        return lax.select_n(here, pages[1][b, level, :, at], pages[0][b, level, :, at])
+
     first = None
     for level in range(DEPTH):
-        if y_first:
-            here = slot_of(served, block, level)[1] == core
-            key_rows = lax.select_n(here, pair_k[0, level], own_k[0, level])
-            value_rows = lax.select_n(here, pair_v[0, level], own_v[0, level])
-        else:
-            key_rows, value_rows = page_k[level, 0], page_v[level, 0]
+        key_rows, value_rows = page_rows(level, 0), page_rows(level, 1)
         live = served[block, level] >= 0
         first = key_rows if level == 0 else first
         rows = slice(level * PAGE, (level + 1) * PAGE)
@@ -204,39 +209,37 @@
         keys[rows, :] = lax.select_n(live, first, key_rows)
         values[rows, :HEAD] = lax.select_n(live, nothing, value_rows)
         values[rows, HEAD:] = lax.select_n(live, nothing, jnp.ones((PAGE, HEAD), jnp.bfloat16))
-    attend(queries, own_keys, own_values, out, keys, values)
+    own = pl.ds(pl.multiple_of(b * BLOCK, BLOCK), BLOCK)
+    attend(
+        queries.at[own, columns(first_head + h, GROUP * HEAD)],
+        pairs.at[own, columns(first_head + h)],
+        pairs.at[own, columns(KV_HEADS + first_head + h)],
+        out,
+        keys,
+        values,
+    )
 
 
 def attention(tok, served, pages, heads, queries, own_pairs, result):
     y_first = len(pages) == 2
-    count, first = len(heads), heads[0]
-    if y_first:
-        page_block = (1, DEPTH, PAGE, HEAD)
-        at = lambda part: pl.BlockSpec(page_block, lambda h, b: (b, 0, 0, part * count + h))
-    else:
-        page_block = (DEPTH, 1, PAGE, HEAD)
-        at = lambda part: pl.BlockSpec(page_block, lambda h, b: (0, b, 0, part * count + h))
-    wide = pl.BlockSpec((BLOCK, GROUP * HEAD), lambda h, b: (b, first + h))
-    own = lambda part: pl.BlockSpec((BLOCK, HEAD), lambda h, b: (b, part * KV_HEADS + first + h))
-    page_args, page_specs = [], []
-    for page in pages:
-        page_args += [page, page]
-        page_specs += [at(0), at(1)]
-    args = [tok, served] + page_args + [queries, own_pairs, own_pairs]
-    specs = [SMEM(), SMEM()] + page_specs + [wide, own(0), own(1)]
+    args = [tok, served, *pages, queries, own_pairs]
+    specs = [SMEM(), SMEM()] + [VMEM()] * (len(args) - 2)
     aliases = {}
     if result is not None:
         aliases = {len(args): 0}
         args.append(result)
         specs.append(pl.BlockSpec(memory_space=pl.ANY))
-    items = count * QB_DEV * GROUP * BLOCK * KEYS
+    items = len(heads) * QB_DEV * GROUP * BLOCK * KEYS
     return pl.pallas_call(
-        functools.partial(attend_kernel, y_first),
-        grid=(count, QB_DEV),
+        functools.partial(attend_kernel, heads, y_first),
+        grid=(len(heads), QB_DEV),
         out_shape=jax.ShapeDtypeStruct(queries.shape, queries.dtype),
         in_specs=specs,
-        out_specs=wide,
-        scratch_shapes=[pltpu.VMEM((KEYS, HEAD), jnp.bfloat16), pltpu.VMEM((KEYS, 2 * HEAD), jnp.bfloat16)],
+        out_specs=pl.BlockSpec((BLOCK, GROUP * HEAD), lambda h, b: (b, heads[0] + h)),
+        scratch_shapes=[
+            pltpu.VMEM((KEYS, HEAD), jnp.bfloat16),
+            pltpu.VMEM((KEYS, 2 * HEAD), jnp.bfloat16),
+        ],
         input_output_aliases=aliases,
         compiler_params=pltpu.CompilerParams(vmem_limit_bytes=24 << 20),
         cost_estimate=pl.CostEstimate(flops=items * 6 * HEAD, transcendentals=items, bytes_accessed=4 << 20),

time: 156 us -> 151 us (0.968)
  local copies, waits for them, and re-layouts: 4.77 us -> 0.11 us
    unnamed x15 -> x5, local copies, waits for them, and re-layouts: 4.77 us -> 0.11 us
  transfers between devices with their start and end apart: 14 -> 14, of which waited for: 8 -> 8; matrix products, arithmetic and copies ran while one was open for 0% -> 0% of each run, Pallas kernels for 7% -> 8%
where the time goes in v1:
time: 151 us
  waiting for transfers between devices  81.9 us (54%)
  starting transfers between devices  48.5 us (32%)
  Pallas kernels  20 us (13%)
    ppermute x4, waiting for transfers between devices, next_section(): return lax.ppermute(x, 'section', [(i, (i + 1) % n) for i in range(n)])  52 us
    ppermute x8, waiting for transfers between devices, within_tok(): return lax.ppermute(x, 'tok', pairs)  29.8 us
    ppermute x8, starting transfers between devices, within_tok(): return lax.ppermute(x, 'tok', pairs)  24.5 us
    pallas_call x2, Pallas kernels, attention(): pl.pallas_call(functools.partial(attend_kernel, heads, y_first), grid=(le...  14.5 us
    all_to_all x2, starting transfers between devices, across_rows(): return lax.all_to_all(x, 'tok', 0, 0, axis_index_groups=columns, tiled=True)  13.3 us
    ppermute x4, starting transfers between devices, next_section(): return lax.ppermute(x, 'section', [(i, (i + 1) % n) for i in range(n)])  10.7 us
  transfers between devices with their start and end apart: 14, of which 8 were waited for; matrix products, arithmetic and copies ran while one was open for 0% of the time, Pallas kernels for 8%

profile of v1, /device:TPU:1, one launch (start us, length us, event | category | flops | bytes accessed | tf_op | source)
XLA Modules:
  0.0 150.7 jit_solution(4377512686812460629)
XLA Ops:
  0.0 4.9 %collective-permute-start.1 = (bf16[64,1024]{1,0:T(8,128)(2,1)}, bf16[64,1024]{1,0:T(8,128)(2,1)S(1)}, u32[]{:S(2)}, u32[]{:S(2)}) collective-permute-start(bf16[64,1024]{1,0:T(8,128)(2,1)} %bitcast.12), channel_id=1, source_target_pairs={{0,64},{64,128},{128,192},{192,256},{256,320},{320,384},{384,448},... | collective-permute-start | bytes 393224 | tf_op jit(solution)/shard_map/ppermute | solution.py:34
  4.9 10.1 %collective-permute-done.1.refs_0_.page = bf16[64,1024]{1,0:T(8,128)(2,1)S(1)} collective-permute-done((bf16[64,1024]{1,0:T(8,128)(2,1)}, bf16[64,1024]{1,0:T(8,128)(2,1)S(1)}, u32[]{:S(2)}, u32[]{:S(2)}) %collective-permute-start.1) | collective-permute-done | bytes 131104 | tf_op jit(solution)/shard_map/ppermute | solution.py:34
  15.0 0.8 shard_map.47
  15.8 6.8 %all-to-all-start.1 = ((bf16[8,64,512]{2,1,0:T(8,128)(2,1)}), bf16[8,64,512]{2,1,0:T(8,128)(2,1)S(1)}, u32[]{:S(2)}, u32[]{:S(2)}) async-start(bf16[8,64,512]{2,1,0:T(8,128)(2,1)} %shard_map.47), calls=%async_computation.1 | async-start | bytes 1048576 | tf_op jit(solution)/shard_map/all_to_all | solution.py:49
  22.7 1.9 %collective-permute-start.6 = (bf16[256,4096]{1,0:T(8,128)(2,1)}, bf16[256,4096]{1,0:T(8,128)(2,1)}, u32[]{:S(2)}, u32[]{:S(2)}) collective-permute-start(bf16[256,4096]{1,0:T(8,128)(2,1)} %bitcast.10), channel_id=1, source_target_pairs={{0,64},{64,128},{128,192},{192,256},{256,320},{320,384},{384,448},... | collective-permute-start | bytes 6291464 | tf_op jit(solution)/shard_map/ppermute | solution.py:34
  24.6 4.4 %collective-permute-start.4 = (bf16[64,1024]{1,0:T(8,128)(2,1)S(1)}, bf16[64,1024]{1,0:T(8,128)(2,1)S(1)}, u32[]{:S(2)}, u32[]{:S(2)}) collective-permute-start(bf16[64,1024]{1,0:T(8,128)(2,1)S(1)} %collective-permute-done.1.refs_0_.page), channel_id=1, source_target_pairs={{0,6},{1,7},{2,0},{3,1},{4,2},{5,3},{6,4},{7,5},{8,14},{9,15},{10,... | collective-permute-start | bytes 393224 | tf_op jit(solution)/shard_map/ppermute | solution.py:44
  29.0 2.4 %collective-permute-start.3 = (bf16[64,1024]{1,0:T(8,128)(2,1)S(1)}, bf16[64,1024]{1,0:T(8,128)(2,1)S(1)}, u32[]{:S(2)}, u32[]{:S(2)}) collective-permute-start(bf16[64,1024]{1,0:T(8,128)(2,1)S(1)} %collective-permute-done.1.refs_0_.page), channel_id=1, source_target_pairs={{0,4},{1,5},{2,6},{3,7},{4,0},{5,1},{6,2},{7,3},{8,12},{9,13},{10,... | collective-permute-start | bytes 393224 | tf_op jit(solution)/shard_map/ppermute | solution.py:44
  31.4 2.5 %collective-permute-start.2 = (bf16[64,1024]{1,0:T(8,128)(2,1)S(1)}, bf16[64,1024]{1,0:T(8,128)(2,1)S(1)}, u32[]{:S(2)}, u32[]{:S(2)}) collective-permute-start(bf16[64,1024]{1,0:T(8,128)(2,1)S(1)} %collective-permute-done.1.refs_0_.page), channel_id=1, source_target_pairs={{0,2},{1,3},{2,4},{3,5},{4,6},{5,7},{6,0},{7,1},{8,10},{9,11},{10,... | collective-permute-start | bytes 393224 | tf_op jit(solution)/shard_map/ppermute | solution.py:44
  33.9 0.0 collective-permute-done.4.refs_3_
  34.0 2.2 %collective-permute-done.3.refs_2_ = bf16[64,1024]{1,0:T(8,128)(2,1)S(1)} collective-permute-done((bf16[64,1024]{1,0:T(8,128)(2,1)S(1)}, bf16[64,1024]{1,0:T(8,128)(2,1)S(1)}, u32[]{:S(2)}, u32[]{:S(2)}) %collective-permute-start.3) | collective-permute-done | bytes 131104 | tf_op jit(solution)/shard_map/ppermute | solution.py:44
  36.2 4.1 %collective-permute-done.2.refs_1_ = bf16[64,1024]{1,0:T(8,128)(2,1)S(1)} collective-permute-done((bf16[64,1024]{1,0:T(8,128)(2,1)S(1)}, bf16[64,1024]{1,0:T(8,128)(2,1)S(1)}, u32[]{:S(2)}, u32[]{:S(2)}) %collective-permute-start.2) | collective-permute-done | bytes 131104 | tf_op jit(solution)/shard_map/ppermute | solution.py:44
  40.3 3.5 %collective-permute-start.5 = (bf16[4,64,512]{2,1,0:T(8,128)(2,1)S(1)}, bf16[4,64,512]{2,1,0:T(8,128)(2,1)S(1)}, u32[]{:S(2)}, u32[]{:S(2)}) collective-permute-start(bf16[4,64,512]{2,1,0:T(8,128)(2,1)S(1)} %shard_map.46.mine), channel_id=1, source_target_pairs={{0,1},{1,0},{2,3},{3,2},{4,5},{5,4},{6,7},{7,6},{8,9},{9,8},{10,11... | collective-permute-start | bytes 786440 | tf_op jit(solution)/shard_map/ppermute | solution.py:44
  43.8 0.1 copy.6
  43.9 1.9 %collective-permute-start = (s32[128,8]{1,0:T(8,128)S(1)}, s32[128,8]{1,0:T(8,128)S(1)}, u32[]{:S(2)}, u32[]{:S(2)}) collective-permute-start(s32[128,8]{1,0:T(8,128)S(1)} %bitcast.9), channel_id=1, source_target_pairs={{0,64},{64,128},{128,192},{192,256},{256,320},{320,384},{384,448},... | collective-permute-start | bytes 12296 | tf_op jit(solution)/shard_map/ppermute | solution.py:34
  45.8 27.3 %collective-permute-done.served = s32[128,8]{1,0:T(8,128)S(1)} collective-permute-done((s32[128,8]{1,0:T(8,128)S(1)}, s32[128,8]{1,0:T(8,128)S(1)}, u32[]{:S(2)}, u32[]{:S(2)}) %collective-permute-start) | collective-permute-done | bytes 4128 | tf_op jit(solution)/shard_map/ppermute | solution.py:34
  73.1 0.0 collective-permute-done.5.other
  73.1 2.7 %pick_for_rows.1 = bf16[8,2,64,512]{3,2,1,0:T(8,128)(2,1)} custom-call(s32[1]{0:T(128)} %bitcast.tok, s32[128,8]{1,0:T(8,128)S(1)} %collective-permute-done.served, bf16[4,64,512]{2,1,0:T(8,128)(2,1)S(1)} %shard_map.46.mine, bf16[4,64,512]{2,1,0:T(8,128)(2,1)S(1)} %collective-permute-done.5.other), custom_call_target="tpu_custom_call" | custom-call | bytes 4194304 | tf_op jit(solution)/shard_map/pick_for_rows/pallas_call | solution.py:104
  75.9 0.0 all-to-all-done.1.from0
  75.9 6.5 %all-to-all-start = ((bf16[8,128,512]{2,1,0:T(8,128)(2,1)}), bf16[8,128,512]{2,1,0:T(8,128)(2,1)S(1)}, u32[]{:S(2)}, u32[]{:S(2)}) async-start(bf16[8,128,512]{2,1,0:T(8,128)(2,1)} %bitcast.3), calls=%async_computation | async-start | bytes 2097152 | tf_op jit(solution)/shard_map/all_to_all | solution.py:49
  82.4 4.4 %collective-permute-start.10 = (bf16[8,64,512]{2,1,0:T(8,128)(2,1)S(1)}, bf16[8,64,512]{2,1,0:T(8,128)(2,1)S(1)}, u32[]{:S(2)}, u32[]{:S(2)}) collective-permute-start(bf16[8,64,512]{2,1,0:T(8,128)(2,1)S(1)} %all-to-all-done.1.from0), channel_id=1, source_target_pairs={{0,6},{1,7},{2,0},{3,1},{4,2},{5,3},{6,4},{7,5},{8,14},{9,15},{10,... | collective-permute-start | bytes 1572872 | tf_op jit(solution)/shard_map/ppermute | solution.py:44
  86.7 2.4 %collective-permute-start.9 = (bf16[8,64,512]{2,1,0:T(8,128)(2,1)S(1)}, bf16[8,64,512]{2,1,0:T(8,128)(2,1)S(1)}, u32[]{:S(2)}, u32[]{:S(2)}) collective-permute-start(bf16[8,64,512]{2,1,0:T(8,128)(2,1)S(1)} %all-to-all-done.1.from0), channel_id=1, source_target_pairs={{0,4},{1,5},{2,6},{3,7},{4,0},{5,1},{6,2},{7,3},{8,12},{9,13},{10,... | collective-permute-start | bytes 1572872 | tf_op jit(solution)/shard_map/ppermute | solution.py:44
  89.2 2.5 %collective-permute-start.8 = (bf16[8,64,512]{2,1,0:T(8,128)(2,1)S(1)}, bf16[8,64,512]{2,1,0:T(8,128)(2,1)S(1)}, u32[]{:S(2)}, u32[]{:S(2)}) collective-permute-start(bf16[8,64,512]{2,1,0:T(8,128)(2,1)S(1)} %all-to-all-done.1.from0), channel_id=1, source_target_pairs={{0,2},{1,3},{2,4},{3,5},{4,6},{5,7},{6,0},{7,1},{8,10},{9,11},{10,... | collective-permute-start | bytes 1572872 | tf_op jit(solution)/shard_map/ppermute | solution.py:44
  91.7 4.3 %collective-permute-done.10.from3 = bf16[8,64,512]{2,1,0:T(8,128)(2,1)S(1)} collective-permute-done((bf16[8,64,512]{2,1,0:T(8,128)(2,1)S(1)}, bf16[8,64,512]{2,1,0:T(8,128)(2,1)S(1)}, u32[]{:S(2)}, u32[]{:S(2)}) %collective-permute-start.10) | collective-permute-done | bytes 524320 | tf_op jit(solution)/shard_map/ppermute | solution.py:44
  96.0 4.6 %collective-permute-done.9.from2 = bf16[8,64,512]{2,1,0:T(8,128)(2,1)S(1)} collective-permute-done((bf16[8,64,512]{2,1,0:T(8,128)(2,1)S(1)}, bf16[8,64,512]{2,1,0:T(8,128)(2,1)S(1)}, u32[]{:S(2)}, u32[]{:S(2)}) %collective-permute-start.9) | collective-permute-done | bytes 524320 | tf_op jit(solution)/shard_map/ppermute | solution.py:44
  100.5 14.7 %collective-permute-done.8.from1 = bf16[8,64,512]{2,1,0:T(8,128)(2,1)S(1)} collective-permute-done((bf16[8,64,512]{2,1,0:T(8,128)(2,1)S(1)}, bf16[8,64,512]{2,1,0:T(8,128)(2,1)S(1)}, u32[]{:S(2)}, u32[]{:S(2)}) %collective-permute-start.8) | collective-permute-done | bytes 524320 | tf_op jit(solution)/shard_map/ppermute | solution.py:44
  115.2 1.9 %pick_for_pair.1 = (bf16[2,8,64,512]{3,2,1,0:T(8,128)(2,1)S(1)}, bf16[2,8,64,512]{3,2,1,0:T(8,128)(2,1)S(1)}) custom-call(s32[1]{0:T(128)} %bitcast.tok, s32[128,8]{1,0:T(8,128)S(1)} %collective-permute-done.served, bf16[8,64,512]{2,1,0:T(8,128)(2,1)S(1)} %all-to-all-done.1.from0, bf16[8,64,512]{2,1,0:T(8,128)(2,1)S(1)} %collective-permute-done.8.from1, ...), custom_call_target="tpu_custom_call" | custom-call | bytes 8388608 | tf_op jit(solution)/shard_map/pick_for_pair/pallas_call | solution.py:129
  117.1 2.4 %collective-permute-start.11 = (bf16[2,8,64,512]{3,2,1,0:T(8,128)(2,1)S(1)}, bf16[2,8,64,512]{3,2,1,0:T(8,128)(2,1)S(1)}, u32[]{:S(2)}, u32[]{:S(2)}) collective-permute-start(bf16[2,8,64,512]{3,2,1,0:T(8,128)(2,1)S(1)} %get-tuple-element.8), channel_id=1, source_target_pairs={{0,1},{1,0},{2,3},{3,2},{4,5},{5,4},{6,7},{7,6},{8,9},{9,8},{10,11... | collective-permute-start | bytes 3145736 | tf_op jit(solution)/shard_map/ppermute | solution.py:44
  119.6 1.9 %collective-permute-start.7 = (bf16[256,1024]{1,0:T(8,128)(2,1)S(1)}, bf16[256,1024]{1,0:T(8,128)(2,1)S(1)}, u32[]{:S(2)}, u32[]{:S(2)}) collective-permute-start(bf16[256,1024]{1,0:T(8,128)(2,1)S(1)} %bitcast.11), channel_id=1, source_target_pairs={{0,64},{64,128},{128,192},{192,256},{256,320},{320,384},{384,448},... | collective-permute-start | bytes 1572872 | tf_op jit(solution)/shard_map/ppermute | solution.py:34
  121.5 14.6 %collective-permute-done.7.refs_3_.refs_2_ = bf16[256,1024]{1,0:T(8,128)(2,1)S(1)} collective-permute-done((bf16[256,1024]{1,0:T(8,128)(2,1)S(1)}, bf16[256,1024]{1,0:T(8,128)(2,1)S(1)}, u32[]{:S(2)}, u32[]{:S(2)}) %collective-permute-start.7) | collective-permute-done | bytes 524320 | tf_op jit(solution)/shard_map/ppermute | solution.py:34
  136.1 0.0 collective-permute-done.6.refs_2_.refs_1_
  136.1 7.3 %attend_b.1.refs_3_ = bf16[256,4096]{1,0:T(8,128)(2,1)} custom-call(s32[1]{0:T(128)} %bitcast.tok, s32[128,8]{1,0:T(8,128)S(1)} %collective-permute-done.served, bf16[2,8,64,512]{3,2,1,0:T(8,128)(2,1)S(1)} %get-tuple-element.7.refs_0_, bf16[2,8,64,512]{3,2,1,0:T(8,128)(2,1)S(1)} %collective-permute-done.11.refs_1_, ...), custom_call_target="tpu_custom_call" | custom-call | flops 2013265920 | bytes 4194304 | tf_op jit(solution)/shard_map/attend_b/pallas_call | solution.py:233
  143.4 7.3 %attend_a.1 = bf16[256,4096]{1,0:T(8,128)(2,1)} custom-call(s32[1]{0:T(128)} %bitcast.tok, s32[128,8]{1,0:T(8,128)S(1)} %collective-permute-done.served, bf16[8,2,64,512]{3,2,1,0:T(8,128)(2,1)S(1)} %bitcast.8, bf16[256,4096]{1,0:T(8,128)(2,1)} %collective-permute-done.6.refs_2_.refs_1_, ...), custom_call_target="tpu_custom_call", output_to_operand_aliasing={{}: (5, {})} | custom-call | flops 2013265920 | bytes 4194304 | tf_op jit(solution)/shard_map/attend_a/pallas_call | solution.py:233
  (7 shorter events, 0.0 us)
Async XLA Ops:
  0.0 43.8 %copy-start = (s32[1,128,8]{1,2,0:T(8,128)S(1)}, s32[1,128,8]{1,2,0:T(8,128)}, u32[]{:S(2)}) copy-start(s32[1,128,8]{1,2,0:T(8,128)} %param.7) | copy-start | bytes 12292
  0.0 15.0 %collective-permute-start.1 = (bf16[64,1024]{1,0:T(8,128)(2,1)}, bf16[64,1024]{1,0:T(8,128)(2,1)S(1)}, u32[]{:S(2)}, u32[]{:S(2)}) collective-permute-start(bf16[64,1024]{1,0:T(8,128)(2,1)} %bitcast.12), channel_id=1, source_target_pairs={{0,64},{64,128},{128,192},{192,256},{256,320},{320,384},{384,448},... | collective-permute-start | bytes 393224 | tf_op jit(solution)/shard_map/ppermute | solution.py:34
  15.8 60.0 %all-to-all-start.1 = ((bf16[8,64,512]{2,1,0:T(8,128)(2,1)}), bf16[8,64,512]{2,1,0:T(8,128)(2,1)S(1)}, u32[]{:S(2)}, u32[]{:S(2)}) async-start(bf16[8,64,512]{2,1,0:T(8,128)(2,1)} %shard_map.47), calls=%async_computation.1 | async-start | bytes 1048576 | tf_op jit(solution)/shard_map/all_to_all | solution.py:49
  22.7 113.5 %collective-permute-start.6 = (bf16[256,4096]{1,0:T(8,128)(2,1)}, bf16[256,4096]{1,0:T(8,128)(2,1)}, u32[]{:S(2)}, u32[]{:S(2)}) collective-permute-start(bf16[256,4096]{1,0:T(8,128)(2,1)} %bitcast.10), channel_id=1, source_target_pairs={{0,64},{64,128},{128,192},{192,256},{256,320},{320,384},{384,448},... | collective-permute-start | bytes 6291464 | tf_op jit(solution)/shard_map/ppermute | solution.py:34
  24.6 9.4 %collective-permute-start.4 = (bf16[64,1024]{1,0:T(8,128)(2,1)S(1)}, bf16[64,1024]{1,0:T(8,128)(2,1)S(1)}, u32[]{:S(2)}, u32[]{:S(2)}) collective-permute-start(bf16[64,1024]{1,0:T(8,128)(2,1)S(1)} %collective-permute-done.1.refs_0_.page), channel_id=1, source_target_pairs={{0,6},{1,7},{2,0},{3,1},{4,2},{5,3},{6,4},{7,5},{8,14},{9,15},{10,... | collective-permute-start | bytes 393224 | tf_op jit(solution)/shard_map/ppermute | solution.py:44
  29.0 7.2 %collective-permute-start.3 = (bf16[64,1024]{1,0:T(8,128)(2,1)S(1)}, bf16[64,1024]{1,0:T(8,128)(2,1)S(1)}, u32[]{:S(2)}, u32[]{:S(2)}) collective-permute-start(bf16[64,1024]{1,0:T(8,128)(2,1)S(1)} %collective-permute-done.1.refs_0_.page), channel_id=1, source_target_pairs={{0,4},{1,5},{2,6},{3,7},{4,0},{5,1},{6,2},{7,3},{8,12},{9,13},{10,... | collective-permute-start | bytes 393224 | tf_op jit(solution)/shard_map/ppermute | solution.py:44
  31.4 8.8 %collective-permute-start.2 = (bf16[64,1024]{1,0:T(8,128)(2,1)S(1)}, bf16[64,1024]{1,0:T(8,128)(2,1)S(1)}, u32[]{:S(2)}, u32[]{:S(2)}) collective-permute-start(bf16[64,1024]{1,0:T(8,128)(2,1)S(1)} %collective-permute-done.1.refs_0_.page), channel_id=1, source_target_pairs={{0,2},{1,3},{2,4},{3,5},{4,6},{5,7},{6,0},{7,1},{8,10},{9,11},{10,... | collective-permute-start | bytes 393224 | tf_op jit(solution)/shard_map/ppermute | solution.py:44
  40.3 32.9 %collective-permute-start.5 = (bf16[4,64,512]{2,1,0:T(8,128)(2,1)S(1)}, bf16[4,64,512]{2,1,0:T(8,128)(2,1)S(1)}, u32[]{:S(2)}, u32[]{:S(2)}) collective-permute-start(bf16[4,64,512]{2,1,0:T(8,128)(2,1)S(1)} %shard_map.46.mine), channel_id=1, source_target_pairs={{0,1},{1,0},{2,3},{3,2},{4,5},{5,4},{6,7},{7,6},{8,9},{9,8},{10,11... | collective-permute-start | bytes 786440 | tf_op jit(solution)/shard_map/ppermute | solution.py:44
  43.9 29.3 %collective-permute-start = (s32[128,8]{1,0:T(8,128)S(1)}, s32[128,8]{1,0:T(8,128)S(1)}, u32[]{:S(2)}, u32[]{:S(2)}) collective-permute-start(s32[128,8]{1,0:T(8,128)S(1)} %bitcast.9), channel_id=1, source_target_pairs={{0,64},{64,128},{128,192},{192,256},{256,320},{320,384},{384,448},... | collective-permute-start | bytes 12296 | tf_op jit(solution)/shard_map/ppermute | solution.py:34
  75.9 43.7 %copy-start.1 = (bf16[1,256,1024]{2,1,0:T(8,128)(2,1)S(1)}, bf16[1,256,1024]{2,1,0:T(8,128)(2,1)}, u32[]{:S(2)}) copy-start(bf16[1,256,1024]{2,1,0:T(8,128)(2,1)} %param.5) | copy-start | bytes 1572868
  75.9 67.6 %all-to-all-start = ((bf16[8,128,512]{2,1,0:T(8,128)(2,1)}), bf16[8,128,512]{2,1,0:T(8,128)(2,1)S(1)}, u32[]{:S(2)}, u32[]{:S(2)}) async-start(bf16[8,128,512]{2,1,0:T(8,128)(2,1)} %bitcast.3), calls=%async_computation | async-start | bytes 2097152 | tf_op jit(solution)/shard_map/all_to_all | solution.py:49
  82.4 13.6 %collective-permute-start.10 = (bf16[8,64,512]{2,1,0:T(8,128)(2,1)S(1)}, bf16[8,64,512]{2,1,0:T(8,128)(2,1)S(1)}, u32[]{:S(2)}, u32[]{:S(2)}) collective-permute-start(bf16[8,64,512]{2,1,0:T(8,128)(2,1)S(1)} %all-to-all-done.1.from0), channel_id=1, source_target_pairs={{0,6},{1,7},{2,0},{3,1},{4,2},{5,3},{6,4},{7,5},{8,14},{9,15},{10,... | collective-permute-start | bytes 1572872 | tf_op jit(solution)/shard_map/ppermute | solution.py:44
  86.7 13.8 %collective-permute-start.9 = (bf16[8,64,512]{2,1,0:T(8,128)(2,1)S(1)}, bf16[8,64,512]{2,1,0:T(8,128)(2,1)S(1)}, u32[]{:S(2)}, u32[]{:S(2)}) collective-permute-start(bf16[8,64,512]{2,1,0:T(8,128)(2,1)S(1)} %all-to-all-done.1.from0), channel_id=1, source_target_pairs={{0,4},{1,5},{2,6},{3,7},{4,0},{5,1},{6,2},{7,3},{8,12},{9,13},{10,... | collective-permute-start | bytes 1572872 | tf_op jit(solution)/shard_map/ppermute | solution.py:44
  89.2 26.0 %collective-permute-start.8 = (bf16[8,64,512]{2,1,0:T(8,128)(2,1)S(1)}, bf16[8,64,512]{2,1,0:T(8,128)(2,1)S(1)}, u32[]{:S(2)}, u32[]{:S(2)}) collective-permute-start(bf16[8,64,512]{2,1,0:T(8,128)(2,1)S(1)} %all-to-all-done.1.from0), channel_id=1, source_target_pairs={{0,2},{1,3},{2,4},{3,5},{4,6},{5,7},{6,0},{7,1},{8,10},{9,11},{10,... | collective-permute-start | bytes 1572872 | tf_op jit(solution)/shard_map/ppermute | solution.py:44
  117.1 19.0 %collective-permute-start.11 = (bf16[2,8,64,512]{3,2,1,0:T(8,128)(2,1)S(1)}, bf16[2,8,64,512]{3,2,1,0:T(8,128)(2,1)S(1)}, u32[]{:S(2)}, u32[]{:S(2)}) collective-permute-start(bf16[2,8,64,512]{3,2,1,0:T(8,128)(2,1)S(1)} %get-tuple-element.8), channel_id=1, source_target_pairs={{0,1},{1,0},{2,3},{3,2},{4,5},{5,4},{6,7},{7,6},{8,9},{9,8},{10,11... | collective-permute-start | bytes 3145736 | tf_op jit(solution)/shard_map/ppermute | solution.py:44
  119.6 16.6 %collective-permute-start.7 = (bf16[256,1024]{1,0:T(8,128)(2,1)S(1)}, bf16[256,1024]{1,0:T(8,128)(2,1)S(1)}, u32[]{:S(2)}, u32[]{:S(2)}) collective-permute-start(bf16[256,1024]{1,0:T(8,128)(2,1)S(1)} %bitcast.11), channel_id=1, source_target_pairs={{0,64},{64,128},{128,192},{192,256},{256,320},{320,384},{384,448},... | collective-permute-start | bytes 1572872 | tf_op jit(solution)/shard_map/ppermute | solution.py:34
